TPU v7x, 32 devices: a whole 2x2x4 slice. The times are simulated.
32 devices in a mesh: group: 4 (over y, x), space: 8 (over z, core).
Axes of the slice: x: 2, y: 2, z: 4, core: 2. Of those that a mesh axis runs over, the one named last changes fastest.
Arguments:
- vectors: bfloat16 [128, 2, 3, 4096], P('group', None, None, 'space'), may hold values from -3 to 3
- momentum: int32 [3], replicated, may hold values from -3 to 3
- assignment: int32 [128], replicated, may hold values from 0 to 127, each once
Outputs:
- elementals: float32 [128, 2, 128, 128], P('space', None, 'group')
Inputs may be any that keep to these rules, and one draw needn't show every extreme that they name: `assignment`: each eigenvector is named by exactly one slot.
All inputs are finite; a program needn't handle non-finite values.
Results may differ from a plain program's by a relative error of at most 0.0029.
Values may be sent and summed in bfloat16 or wider, within the bound.
A program may use at most 128 MiB of HBM per device.

v0:
```python
import math

import jax
import jax.numpy as jnp
from jax import lax
from jax.sharding import PartitionSpec as P

L = 64


def complex_product(left_re, left_im, right_re, right_im):
    return (left_re * right_re - left_im * right_im, left_re * right_im + left_im * right_re)


def weighted_slot(vec32, slot_vec, cosine, sine):
    crosses_re = []
    crosses_im = []
    for colour in range(3):
        second = (colour + 1) % 3
        third = (colour + 2) % 3
        one_re, one_im = complex_product(
            vec32[:, 0, second], vec32[:, 1, second], slot_vec[0, third], slot_vec[1, third]
        )
        two_re, two_im = complex_product(
            vec32[:, 0, third], vec32[:, 1, third], slot_vec[0, second], slot_vec[1, second]
        )
        cross_re = one_re - two_re
        cross_im = one_im - two_im
        crosses_re.append(cross_re * cosine - cross_im * sine)
        crosses_im.append(cross_re * sine + cross_im * cosine)
    stacked = jnp.stack([jnp.stack(crosses_re, axis=1), jnp.stack(crosses_im, axis=1)], axis=1)
    return stacked.astype(jnp.bfloat16)


def local(vectors, momentum, assignment):
    block_size = vectors.shape[0]
    site_count = vectors.shape[3]
    space_size = lax.axis_size("space")
    total_sites = site_count * space_size
    gathered = lax.all_gather(vectors, "group", axis=0, tiled=True)
    total_vecs = gathered.shape[0]
    sites = lax.axis_index("space") * site_count + jnp.arange(site_count, dtype=jnp.int32)
    coord_x = sites % L
    coord_y = sites // L % L
    coord_z = sites // (L * L)
    phase_index = jnp.mod(momentum[0] * coord_x + momentum[1] * coord_y + momentum[2] * coord_z, L)
    angle = phase_index.astype(jnp.float32) * jnp.float32(2.0 * math.pi / L)
    cosine = jnp.cos(angle)
    sine = jnp.sin(angle)
    slot_ids = lax.dynamic_slice_in_dim(
        assignment, lax.axis_index("group") * block_size, block_size
    )
    vec32 = gathered.astype(jnp.float32)

    def one_slot(index):
        slot_vec = jnp.take(vec32, index, axis=0)
        return weighted_slot(vec32, slot_vec, cosine, sine)

    weighted = lax.map(one_slot, slot_ids).reshape(block_size * total_vecs, 2, 3 * site_count)
    flat_left = gathered.reshape(total_vecs, 2, 3 * site_count)
    scale = jnp.float32(1.0 / math.sqrt(total_sites))
    row_count = total_vecs // space_size
    products = jnp.einsum("ipx,mqx->ipqm", flat_left, weighted, preferred_element_type=jnp.float32)
    real_part = products[:, 0, 0] - products[:, 1, 1]
    imag_part = products[:, 0, 1] + products[:, 1, 0]
    joined = jnp.stack([real_part, imag_part], axis=1)
    summed = lax.psum(joined.reshape(total_vecs, 2, block_size, total_vecs) * scale, "space")
    return lax.dynamic_slice_in_dim(summed, lax.axis_index("space") * row_count, row_count, 0)


def solution(mesh):
    placed = (P("group", None, None, "space"), P(), P())
    return jax.shard_map(
        local,
        mesh=mesh,
        in_specs=placed,
        out_specs=P("space", None, "group", None),
        check_vma=False,
    )
```

profile of v0, /device:TPU:0, one launch (start us, length us, event | category | flops | bytes accessed | tf_op | source)
XLA Modules:
  0.0 420.4 jit_solution(16571338819917680055)
XLA Ops:
  6.5 13.9 %all_gather.3 = bf16[128,2,3,512]{3,1,2,0:T(2,128)(2,1)S(1)} all-gather(bf16[32,2,3,512]{3,1,2,0:T(2,128)(2,1)} %param.5), channel_id=1, replica_groups=mesh['group'=4,'space'=8] {'group'}, dimensions={0}, use_global_device_ids=true | all-gather | bytes 983040 | tf_op jit(solution)/shard_map/all_gather | solution.py:40
  22.3 197.2 %while.13 = (s32[]{:T(128)}, bf16[32,128,2,3,512]{4,1,3,2,0:T(8,128)(2,1)}, f32[128,2,3,512]{3,0,2,1:T(8,128)S(1)}, s32[32]{0:T(128)S(1)}, s32[]{:T(128)}, /*ind...) while((s32[]{:T(128)}, ...), condition=%wide.region_1.2_spmd.clone.clone, body=%wide.region_0.1_spmd.clone.clone.sunk | while | flops 6717960 | bytes 9810637 | solution.py:59
  24.6 2.1 fusion.48
  30.8 2.1 fusion.48
  36.9 2.1 fusion.48
  43.1 2.1 fusion.48
  49.2 2.1 fusion.48
  55.4 2.1 fusion.48
  61.5 2.1 fusion.48
  64.3 1.0 maximum_dynamic-update-slice_fusion.2
  67.7 2.1 fusion.48
  73.8 2.1 fusion.48
  80.0 2.1 fusion.48
  86.1 2.1 fusion.48
  89.0 1.1 maximum_dynamic-update-slice_fusion.2
  92.4 2.1 fusion.48
  95.2 1.1 maximum_dynamic-update-slice_fusion.2
  98.6 2.1 fusion.48
  104.7 2.1 fusion.48
  110.9 2.1 fusion.48
  117.1 2.1 fusion.48
  123.2 2.1 fusion.48
  126.1 1.0 maximum_dynamic-update-slice_fusion.2
  129.4 2.1 fusion.48
  135.6 2.1 fusion.48
  141.8 2.1 fusion.48
  147.9 2.1 fusion.48
  154.1 2.1 fusion.48
  160.2 2.1 fusion.48
  166.4 2.1 fusion.48
  172.6 2.1 fusion.48
  178.7 2.1 fusion.48
  184.8 2.1 fusion.48
  191.0 2.1 fusion.48
  197.1 2.1 fusion.48
  203.3 2.1 fusion.48
  209.5 2.1 fusion.48
  215.6 2.1 fusion.48
  218.4 1.0 maximum_dynamic-update-slice_fusion.2
  219.5 33.5 %copy.33 = bf16[32,128,2,3,512]{1,0,4,3,2:T(8,128)(2,1)} copy(bf16[32,128,2,3,512]{4,1,3,2,0:T(8,128)(2,1)} %get-tuple-element.37) | data formatting | bytes 50331648 | tf_op jit(solution)/shard_map/while | solution.py:59
  253.0 37.4 %reshape.2091 = bf16[4096,2,1536,1]{0,2,3,1:T(8,128)(2,1)} reshape(bf16[32,128,2,3,512]{1,0,4,3,2:T(8,128)(2,1)} %copy.33) | data formatting | bytes 50331648 | tf_op jit(solution)/shard_map/reshape | solution.py:59
  290.3 12.7 %convolution_bitcast_fusion = f32[128,2,2,4096]{0,3,1,2:T(8,128)S(1)} fusion(bf16[4096,2,1536,1]{0,2,3,1:T(8,128)(2,1)} %reshape.2091, bf16[128,2,1536,1]{0,2,1,3:T(8,128)(2,1)S(1)} %bitcast.179), kind=kOutput, calls=%fused_computation.85 | convolution fusion | flops 6442450944 | bytes 34340864 | tf_op jit(solution)/shard_map/ipx,mqx->ipqm/dot_general | solution.py:63
  303.0 1.8 slice_subtract_fusion
  304.8 3.2 copy.37
  307.9 2.0 copy.38
  310.0 4.8 %maximum_multiply_fusion = f32[128,2,32,128]{3,2,1,0:T(8,128)} fusion(f32[128,1,32,128]{3,2,1,0:T(8,128)} %copy.38, f32[128,1,32,128]{3,2,1,0:T(8,128)} %copy.37), kind=kLoop, calls=%fused_computation.86 | loop fusion | flops 2097152 | bytes 8388608 | tf_op jit(solution)/shard_map/mul | solution.py:67
  314.8 96.9 %all-reduce.2.cloned.1.call-done = f32[128,2,32,128]{3,2,1,0:T(8,128)} async-done(((f32[128,2,32,128]{3,2,1,0:T(8,128)}), f32[128,2,32,128]{3,2,1,0:T(8,128)}) %all-reduce.2.cloned.1.call-update) | async-done | bytes 4194320 | tf_op jit(solution)/shard_map/psum | solution.py:67
  411.7 1.9 constant_dynamic-slice_fusion
  (326 shorter events, 71.2 us)
Async XLA Ops:
  6.5 15.0 %copy-start = (s32[3]{0:T(128)S(1)}, s32[3]{0:T(128)}, u32[]{:S(2)}) copy-start(s32[3]{0:T(128)} %param.6) | copy-start | bytes 40
  6.5 15.7 %copy-start.1 = (s32[128]{0:T(128)S(1)}, s32[128]{0:T(128)}, u32[]{:S(2)}) copy-start(s32[128]{0:T(128)} %param.7) | copy-start | bytes 1540
  6.5 405.2 %all-reduce.2.cloned.1.call-start = ((), (), s32[]{:S(2)}) async-start(), calls=%async_computation | async-start | bytes 8388608 | tf_op jit(solution)/shard_map/psum | solution.py:67
Sparse Core Ops, SparseCore 0:
  314.9 96.7 all-reduce.1
where the time goes:
time: 424 us; the launch traced here: 420 us
  other arithmetic  129 us (30%)
  local copies, waits for them, and re-layouts  98.1 us (23%)
  waiting for transfers between devices  97 us (23%)
  loops' own time  56.6 us (13%)
  blocking collectives  13.9 us (3%)
  between operations  13.4 us (3%)
  matrix products  12.7 us (3%)
    psum x1, waiting for transfers between devices, local(): lax.psum(joined.reshape(total_vecs, 2, block_size, total_vecs) * scale, '...  96.9 us
    sin x32, other arithmetic, local(): sine = jnp.sin(angle)  65.9 us
    another operation x1, loops' own time, local(): lax.map(one_slot, slot_ids)  56.6 us
    reshape x1, local copies, waits for them, and re-layouts, local(): lax.map(one_slot, slot_ids)  37.4 us
    while x1, local copies, waits for them, and re-layouts, local(): lax.map(one_slot, slot_ids)  33.5 us
    dynamic_update_slice x32, other arithmetic, local(): lax.map(one_slot, slot_ids)  31.7 us
    another operation x96, other arithmetic  20.9 us
    dynamic_slice x32, local copies, waits for them, and re-layouts, local(): lax.map(one_slot, slot_ids)  17.8 us
  transfers between devices with their start and end apart: 1, of which 1 were waited for; matrix products, arithmetic and copies ran while one was open for 0% of the time, Pallas kernels for 0%

commit v1 on v0

v1 whole, which is shorter than its diff:
```python
import functools
import math

import jax
import jax.numpy as jnp
from jax import lax
from jax.experimental import pallas as pl
from jax.experimental.pallas import tpu as pltpu
from jax.sharding import PartitionSpec as P

L = 64
MESH = pl.DeviceIdType.MESH
LANES = 128
ROWS = 16


def kernel(
    groups,
    spaces,
    slots_ref,
    momentum_ref,
    block_ref,
    out_ref,
    gathered,
    wide,
    left,
    weighted,
    part,
    part_in,
    rounded,
    rounded_in,
    local_sem,
    gather_send,
    gather_recv,
    pair_send,
    pair_recv,
    sum_send,
    sum_recv,
):
    block = block_ref.shape[1]
    site_count = block_ref.shape[2]
    total = groups * block
    rows = total // spaces
    planes = spaces // 2
    steps = block // 2
    span = 3 * site_count
    scale = jnp.float32(1.0 / math.sqrt(site_count * spaces))
    group = lax.axis_index("group")
    space = lax.axis_index("space")
    core = lax.rem(space, 2)
    plane = lax.div(space, 2)

    barrier = pltpu.get_barrier_semaphore()
    for off in range(1, groups):
        pl.semaphore_signal(
            barrier, inc=1, device_id={"group": lax.rem(group + off, groups)}, device_id_type=MESH
        )
    for off in range(1, planes):
        pl.semaphore_signal(
            barrier,
            inc=1,
            device_id={"space": lax.rem(plane + off, planes) * 2 + core},
            device_id_type=MESH,
        )
    pl.semaphore_signal(
        barrier, inc=1, device_id={"space": plane * 2 + 1 - core}, device_id_type=MESH
    )
    pl.semaphore_wait(barrier, groups + planes - 1)

    sends = []
    for off in range(1, groups):
        copy = pltpu.make_async_remote_copy(
            src_ref=block_ref,
            dst_ref=gathered.at[group],
            send_sem=gather_send.at[off - 1],
            recv_sem=gather_recv.at[off - 1],
            device_id={"group": lax.rem(group + off, groups)},
            device_id_type=MESH,
        )
        copy.start()
        sends.append(copy)
    own = pltpu.make_async_copy(block_ref, gathered.at[group], local_sem)
    own.start()

    sites = space * site_count + lax.broadcasted_iota(jnp.int32, (8, site_count), 1)
    coord_x = sites & (L - 1)
    coord_y = (sites >> 6) & (L - 1)
    coord_z = sites >> 12
    phase = momentum_ref[0] * coord_x + momentum_ref[1] * coord_y + momentum_ref[2] * coord_z
    angle = (phase & (L - 1)).astype(jnp.float32) * jnp.float32(2.0 * math.pi / L)
    cosine = jnp.cos(angle)[0:1]
    sine = jnp.sin(angle)[0:1]

    own.wait()
    for copy in sends:
        copy.wait()

    for q in range(groups):
        for c in range(6):
            wide[c, q * block : (q + 1) * block, :] = gathered[q, c].astype(jnp.float32)

    order = [(2 * z + h) * rows for h in range(2) for z in range(planes)]
    for a in range(3):
        real = wide[a]
        imag = wide[3 + a]
        first = [piece for i in order for piece in (real[i : i + rows], imag[i : i + rows])]
        second = [piece for i in order for piece in (-imag[i : i + rows], real[i : i + rows])]
        low, high = a * site_count, (a + 1) * site_count
        left[:, low:high] = jnp.concatenate(first, axis=0).astype(jnp.bfloat16)
        left[:, span + low : span + high] = jnp.concatenate(second, axis=0).astype(jnp.bfloat16)

    def fill(step):
        for half in range(2):
            k = slots_ref[group * block + 2 * step + half]
            row = [wide[c, pl.ds(k, 1), :] for c in range(6)]
            turn_re = [row[a] * cosine - row[3 + a] * sine for a in range(3)]
            turn_im = [row[a] * sine + row[3 + a] * cosine for a in range(3)]

            def tile(j, carry):
                top = pl.multiple_of(j * ROWS, ROWS)
                for s in range(0, site_count, LANES):
                    cols = slice(s, s + LANES)
                    re = [wide[a, pl.ds(top, ROWS), cols] for a in range(3)]
                    im = [wide[3 + a, pl.ds(top, ROWS), cols] for a in range(3)]
                    tr = [x[:, cols] for x in turn_re]
                    ti = [x[:, cols] for x in turn_im]
                    for a in range(3):
                        b, c = (a + 1) % 3, (a + 2) % 3
                        out_re = (re[b] * tr[c] - im[b] * ti[c]) - (re[c] * tr[b] - im[c] * ti[b])
                        out_im = (re[b] * ti[c] + im[b] * tr[c]) - (re[c] * ti[b] + im[c] * tr[b])
                        base = a * site_count + s
                        at = pl.ds(half * total + top, ROWS)
                        weighted[at, base : base + LANES] = out_re.astype(jnp.bfloat16)
                        weighted[at, span + base : span + base + LANES] = out_im.astype(jnp.bfloat16)
                return carry

            lax.fori_loop(0, total // ROWS, tile, 0, unroll=True)

    def pair_copy(step):
        return pltpu.make_async_remote_copy(
            src_ref=part.at[step, 1 - core],
            dst_ref=part_in.at[step],
            send_sem=pair_send.at[step],
            recv_sem=pair_recv.at[step],
            device_id={"space": plane * 2 + 1 - core},
            device_id_type=MESH,
        )

    def sum_copy(step, off):
        target = lax.rem(plane + off, planes)
        return pltpu.make_async_remote_copy(
            src_ref=rounded.at[step, target],
            dst_ref=rounded_in.at[off - 1, step],
            send_sem=sum_send.at[off - 1, step],
            recv_sem=sum_recv.at[off - 1, step],
            device_id={"space": target * 2 + core},
            device_id_type=MESH,
        )

    def forward(step):
        pair_copy(step).wait()
        rounded[step] = (part[step, core] + part_in[step]).astype(jnp.bfloat16)
        for off in range(1, planes):
            sum_copy(step, off).start()
        out_ref[pl.ds(2 * step, 2)] = part[step, core, plane] + part_in[step, plane]

    def body(step, carry):
        fill(step)
        product = lax.dot_general(
            left[...], weighted[...], (((1,), (1,)), ((), ())), preferred_element_type=jnp.float32
        )
        for half in range(2):
            piece = product[:, half * total : (half + 1) * total]
            part[step, :, :, half] = piece.reshape(2, planes, 2 * rows, total)
        pair_copy(step).start()

        @pl.when(step >= 1)
        def _():
            forward(step - 1)

        return carry

    lax.fori_loop(0, steps, body, 0)
    forward(steps - 1)

    def finish(step, carry):
        value = out_ref[pl.ds(2 * step, 2)]
        for off in range(1, planes):
            sum_copy(step, off).wait()
            value = value + rounded_in[off - 1, step].astype(jnp.float32)
        out_ref[pl.ds(2 * step, 2)] = value * scale
        return carry

    lax.fori_loop(0, steps, finish, 0)


def local(groups, spaces, vectors, momentum, assignment):
    block, _, _, site_count = vectors.shape
    total = block * groups
    rows = total // spaces
    planes = spaces // 2
    steps = block // 2
    mine = jnp.transpose(vectors, (1, 2, 0, 3)).reshape(6, block, site_count)
    dma = pltpu.SemaphoreType.DMA
    out = pl.pallas_call(
        functools.partial(kernel, groups, spaces),
        out_shape=jax.ShapeDtypeStruct((block, 2 * rows, total), jnp.float32),
        in_specs=[
            pl.BlockSpec(memory_space=pltpu.SMEM),
            pl.BlockSpec(memory_space=pltpu.SMEM),
            pl.BlockSpec(memory_space=pltpu.VMEM),
        ],
        out_specs=pl.BlockSpec(memory_space=pltpu.VMEM),
        scratch_shapes=[
            pltpu.VMEM((groups, 6, block, site_count), jnp.bfloat16),
            pltpu.VMEM((6, total, site_count), jnp.float32),
            pltpu.VMEM((2 * total, 6 * site_count), jnp.bfloat16),
            pltpu.VMEM((2 * total, 6 * site_count), jnp.bfloat16),
            pltpu.VMEM((steps, 2, planes, 2, 2 * rows, total), jnp.float32),
            pltpu.VMEM((steps, planes, 2, 2 * rows, total), jnp.float32),
            pltpu.VMEM((steps, planes, 2, 2 * rows, total), jnp.bfloat16),
            pltpu.VMEM((planes - 1, steps, 2, 2 * rows, total), jnp.bfloat16),
            dma,
            dma((groups - 1,)),
            dma((groups - 1,)),
            dma((steps,)),
            dma((steps,)),
            dma((planes - 1, steps)),
            dma((planes - 1, steps)),
        ],
        compiler_params=pltpu.CompilerParams(
            collective_id=0, has_side_effects=True, vmem_limit_bytes=48 * 1024 * 1024
        ),
    )(assignment, momentum, mine)
    return jnp.transpose(out.reshape(block, 2, rows, total), (2, 1, 0, 3))


def solution(mesh):
    return jax.shard_map(
        functools.partial(local, mesh.shape["group"], mesh.shape["space"]),
        mesh=mesh,
        in_specs=(P("group", None, None, "space"), P(), P()),
        out_specs=P("space", None, "group", None),
        check_vma=False,
    )
```

time: 424 us -> 49.1 us (0.12)
  other arithmetic: 129 us -> 0 us
  waiting for transfers between devices: 97 us -> 0 us
  local copies, waits for them, and re-layouts: 98.1 us -> 2.71 us
  loops' own time: 56.6 us -> 0 us
  Pallas kernels: 0 us -> 46.2 us
  blocking collectives: 13.9 us -> 0 us
  between operations: 13.4 us -> 0.03 us
  matrix products: 12.7 us -> 0 us
    psum x1 -> x0, waiting for transfers between devices: 96.9 us -> none  [local(): lax.psum(joined.reshape(total_vecs, 2, block_size, total_vecs) * scale, '...]
    sin x32 -> x0, other arithmetic: 65.9 us -> none  [local(): sine = jnp.sin(angle)]
    another operation x1 -> x0, loops' own time: 56.6 us -> none  [local(): lax.map(one_slot, slot_ids)]
    pallas_call x0 -> x1, Pallas kernels: none -> 46.2 us  [local(): pl.pallas_call(functools.partial(kernel, groups, spaces), out_shape=jax.S...]
    reshape x1, local copies, waits for them, and re-layouts: 37.4 us -> 1.1 us  [local(): return jnp.transpose(out.reshape(block, 2, rows, total), (2, 1, 0, 3))]
    while x1 -> x0, local copies, waits for them, and re-layouts: 33.5 us -> none  [local(): lax.map(one_slot, slot_ids)]
    dynamic_update_slice x32 -> x0, other arithmetic: 31.7 us -> none  [local(): lax.map(one_slot, slot_ids)]
    another operation x160 -> x0, other arithmetic: 23.9 us -> none
  transfers between devices with their start and end apart: 1 -> 0, of which waited for: 1 -> 0; matrix products, arithmetic and copies ran while one was open for 0% -> 0% of each run, Pallas kernels for 0% -> 0%
where the time goes in v1:
time: 49.1 us; the launch traced here: 48.9 us
  Pallas kernels  46.2 us (94%)
  local copies, waits for them, and re-layouts  2.71 us (6%)
    pallas_call x1, Pallas kernels, local(): pl.pallas_call(functools.partial(kernel, groups, spaces), out_shape=jax.S...  46.2 us
    reshape x1, local copies, waits for them, and re-layouts, local(): return jnp.transpose(out.reshape(block, 2, rows, total), (2, 1, 0, 3))  1.1 us

profile of v1, /device:TPU:0, one launch (start us, length us, event | category | flops | bytes accessed | tf_op | source)
XLA Modules:
  0.0 48.9 jit_solution(13354372357673089812)
XLA Ops:
  0.0 0.9 %copy.4 = bf16[2,3,32,512]{3,2,1,0:T(8,128)(2,1)S(1)} copy(bf16[2,3,32,512]{3,0,1,2:T(2,128)(2,1)} %bitcast.8) | data formatting | bytes 393216 | tf_op jit(solution)/shard_map/transpose | solution.py:203
  1.0 0.0 copy-start
  1.0 0.0 copy-start.1
  1.0 0.6 %copy-done = s32[128]{0:T(128)S(1)} copy-done((s32[128]{0:T(128)S(1)}, s32[128]{0:T(128)}, u32[]{:S(2)}) %copy-start) | copy-done | bytes 536
  1.6 0.0 copy-done.1
  1.6 46.2 %shard_map.37 = f32[32,32,128]{2,1,0:T(8,128)S(1)} custom-call(s32[128]{0:T(128)S(1)} %copy-done, s32[3]{0:T(128)S(1)} %copy-done.1, bf16[6,32,512]{2,1,0:T(8,128)(2,1)S(1)} %bitcast.7), custom_call_target="tpu_custom_call" | custom-call | tf_op jit(solution)/shard_map/pallas_call | solution.py:205
  47.8 1.1 %copy.7 = f32[32,2,16,128]{3,0,1,2:T(8,128)} copy(f32[32,2,16,128]{3,2,1,0:T(8,128)S(1)} %bitcast.6) | data formatting | bytes 1048576 | tf_op jit(solution)/shard_map/reshape | solution.py:235
Async XLA Ops:
  1.0 0.7 %copy-start = (s32[128]{0:T(128)S(1)}, s32[128]{0:T(128)}, u32[]{:S(2)}) copy-start(s32[128]{0:T(128)} %slots_ref.1) | copy-start | bytes 1540
  1.0 0.7 %copy-start.1 = (s32[3]{0:T(128)S(1)}, s32[3]{0:T(128)}, u32[]{:S(2)}) copy-start(s32[3]{0:T(128)} %momentum_ref.1) | copy-start | bytes 40

commit v2 on v1

--- a/solution.py
+++ b/solution.py
@@ -12,6 +12,7 @@
 MESH = pl.DeviceIdType.MESH
 LANES = 128
 ROWS = 16
+SLOTS = 4
 
 
 def kernel(
@@ -23,7 +24,7 @@
     out_ref,
     gathered,
     wide,
-    left,
+    right,
     weighted,
     part,
     part_in,
@@ -42,7 +43,7 @@
     total = groups * block
     rows = total // spaces
     planes = spaces // 2
-    steps = block // 2
+    steps = block // SLOTS
     span = 3 * site_count
     scale = jnp.float32(1.0 / math.sqrt(site_count * spaces))
     group = lax.axis_index("group")
@@ -67,20 +68,44 @@
     )
     pl.semaphore_wait(barrier, groups + planes - 1)
 
-    sends = []
-    for off in range(1, groups):
-        copy = pltpu.make_async_remote_copy(
-            src_ref=block_ref,
-            dst_ref=gathered.at[group],
-            send_sem=gather_send.at[off - 1],
-            recv_sem=gather_recv.at[off - 1],
-            device_id={"group": lax.rem(group + off, groups)},
-            device_id_type=MESH,
-        )
+    def gather_copy(lane, target, source, owner, first, count):
+        at = pl.ds(first, count)
+        return pltpu.make_async_remote_copy(
+            src_ref=source.at[at],
+            dst_ref=gathered.at[owner, at],
+            send_sem=gather_send.at[lane],
+            recv_sem=gather_recv.at[lane],
+            device_id={"group": target},
+            device_id_type=MESH,
+        )
+
+    square = groups == 4
+    if square:
+        beside = group + 1 - 2 * lax.rem(group, 2)
+        across = group + 2 - 4 * lax.div(group, 2)
+        sends = [
+            gather_copy(0, beside, block_ref, group, 0, 3),
+            gather_copy(1, across, block_ref, group, 3, 3),
+            gather_copy(2, beside, block_ref, group, 3, 3),
+            gather_copy(3, across, block_ref, group, 0, 3),
+        ]
+        passed = [
+            gather_copy(4, across, gathered.at[beside], beside, 0, 3),
+            gather_copy(5, beside, gathered.at[across], across, 3, 3),
+        ]
+    else:
+        sends = [
+            gather_copy(off - 1, lax.rem(group + off, groups), block_ref, group, 0, 6)
+            for off in range(1, groups)
+        ]
+    for copy in sends:
         copy.start()
-        sends.append(copy)
     own = pltpu.make_async_copy(block_ref, gathered.at[group], local_sem)
     own.start()
+    if square:
+        for copy, onward in zip(sends, passed):
+            copy.wait_recv()
+            onward.start()
 
     sites = space * site_count + lax.broadcasted_iota(jnp.int32, (8, site_count), 1)
     coord_x = sites & (L - 1)
@@ -92,8 +117,14 @@
     sine = jnp.sin(angle)[0:1]
 
     own.wait()
-    for copy in sends:
-        copy.wait()
+    if square:
+        for copy in sends[:2]:
+            copy.wait_send()
+        for copy in sends[2:] + passed:
+            copy.wait()
+    else:
+        for copy in sends:
+            copy.wait()
 
     for q in range(groups):
         for c in range(6):
@@ -106,17 +137,17 @@
         first = [piece for i in order for piece in (real[i : i + rows], imag[i : i + rows])]
         second = [piece for i in order for piece in (-imag[i : i + rows], real[i : i + rows])]
         low, high = a * site_count, (a + 1) * site_count
-        left[:, low:high] = jnp.concatenate(first, axis=0).astype(jnp.bfloat16)
-        left[:, span + low : span + high] = jnp.concatenate(second, axis=0).astype(jnp.bfloat16)
+        right[low:high] = jnp.concatenate(first, axis=0).T.astype(jnp.bfloat16)
+        right[span + low : span + high] = jnp.concatenate(second, axis=0).T.astype(jnp.bfloat16)
 
     def fill(step):
-        for half in range(2):
-            k = slots_ref[group * block + 2 * step + half]
+        def one(half, carry):
+            k = slots_ref[group * block + SLOTS * step + half]
             row = [wide[c, pl.ds(k, 1), :] for c in range(6)]
             turn_re = [row[a] * cosine - row[3 + a] * sine for a in range(3)]
             turn_im = [row[a] * sine + row[3 + a] * cosine for a in range(3)]
 
-            def tile(j, carry):
+            def tile(j, inner):
                 top = pl.multiple_of(j * ROWS, ROWS)
                 for s in range(0, site_count, LANES):
                     cols = slice(s, s + LANES)
@@ -129,12 +160,14 @@
                         out_re = (re[b] * tr[c] - im[b] * ti[c]) - (re[c] * tr[b] - im[c] * ti[b])
                         out_im = (re[b] * ti[c] + im[b] * tr[c]) - (re[c] * ti[b] + im[c] * tr[b])
                         base = a * site_count + s
-                        at = pl.ds(half * total + top, ROWS)
+                        at = pl.ds(pl.multiple_of(half * total + top, ROWS), ROWS)
                         weighted[at, base : base + LANES] = out_re.astype(jnp.bfloat16)
                         weighted[at, span + base : span + base + LANES] = out_im.astype(jnp.bfloat16)
-                return carry
-
-            lax.fori_loop(0, total // ROWS, tile, 0, unroll=True)
+                return inner
+
+            return lax.fori_loop(0, total // ROWS, tile, carry, unroll=True)
+
+        lax.fori_loop(0, SLOTS, one, 0)
 
     def pair_copy(step):
         return pltpu.make_async_remote_copy(
@@ -162,15 +195,13 @@
         rounded[step] = (part[step, core] + part_in[step]).astype(jnp.bfloat16)
         for off in range(1, planes):
             sum_copy(step, off).start()
-        out_ref[pl.ds(2 * step, 2)] = part[step, core, plane] + part_in[step, plane]
+        out_ref[pl.ds(SLOTS * step, SLOTS)] = part[step, core, plane] + part_in[step, plane]
 
     def body(step, carry):
         fill(step)
-        product = lax.dot_general(
-            left[...], weighted[...], (((1,), (1,)), ((), ())), preferred_element_type=jnp.float32
-        )
-        for half in range(2):
-            piece = product[:, half * total : (half + 1) * total]
+        product = jnp.dot(weighted[...], right[...], preferred_element_type=jnp.float32)
+        for half in range(SLOTS):
+            piece = product[half * total : (half + 1) * total].T
             part[step, :, :, half] = piece.reshape(2, planes, 2 * rows, total)
         pair_copy(step).start()
 
@@ -184,11 +215,11 @@
     forward(steps - 1)
 
     def finish(step, carry):
-        value = out_ref[pl.ds(2 * step, 2)]
+        value = out_ref[pl.ds(SLOTS * step, SLOTS)]
         for off in range(1, planes):
             sum_copy(step, off).wait()
             value = value + rounded_in[off - 1, step].astype(jnp.float32)
-        out_ref[pl.ds(2 * step, 2)] = value * scale
+        out_ref[pl.ds(SLOTS * step, SLOTS)] = value * scale
         return carry
 
     lax.fori_loop(0, steps, finish, 0)
@@ -199,7 +230,7 @@
     total = block * groups
     rows = total // spaces
     planes = spaces // 2
-    steps = block // 2
+    steps = block // SLOTS
     mine = jnp.transpose(vectors, (1, 2, 0, 3)).reshape(6, block, site_count)
     dma = pltpu.SemaphoreType.DMA
     out = pl.pallas_call(
@@ -214,15 +245,15 @@
         scratch_shapes=[
             pltpu.VMEM((groups, 6, block, site_count), jnp.bfloat16),
             pltpu.VMEM((6, total, site_count), jnp.float32),
-            pltpu.VMEM((2 * total, 6 * site_count), jnp.bfloat16),
-            pltpu.VMEM((2 * total, 6 * site_count), jnp.bfloat16),
-            pltpu.VMEM((steps, 2, planes, 2, 2 * rows, total), jnp.float32),
-            pltpu.VMEM((steps, planes, 2, 2 * rows, total), jnp.float32),
-            pltpu.VMEM((steps, planes, 2, 2 * rows, total), jnp.bfloat16),
-            pltpu.VMEM((planes - 1, steps, 2, 2 * rows, total), jnp.bfloat16),
+            pltpu.VMEM((6 * site_count, 2 * total), jnp.bfloat16),
+            pltpu.VMEM((SLOTS * total, 6 * site_count), jnp.bfloat16),
+            pltpu.VMEM((steps, 2, planes, SLOTS, 2 * rows, total), jnp.float32),
+            pltpu.VMEM((steps, planes, SLOTS, 2 * rows, total), jnp.float32),
+            pltpu.VMEM((steps, planes, SLOTS, 2 * rows, total), jnp.bfloat16),
+            pltpu.VMEM((planes - 1, steps, SLOTS, 2 * rows, total), jnp.bfloat16),
             dma,
-            dma((groups - 1,)),
-            dma((groups - 1,)),
+            dma((max(groups - 1, 6),)),
+            dma((max(groups - 1, 6),)),
             dma((steps,)),
             dma((steps,)),
             dma((planes - 1, steps)),

time: 49.1 us -> 47.2 us (0.961)
  Pallas kernels: 46.2 us -> 44.3 us
    pallas_call x1, Pallas kernels: 46.2 us -> 44.3 us  [local(): pl.pallas_call(functools.partial(kernel, groups, spaces), out_shape=jax.S...]
where the time goes in v2:
time: 47.2 us; the launch traced here: 47.1 us
  Pallas kernels  44.3 us (94%)
  local copies, waits for them, and re-layouts  2.71 us (6%)
    pallas_call x1, Pallas kernels, local(): pl.pallas_call(functools.partial(kernel, groups, spaces), out_shape=jax.S...  44.3 us
    reshape x1, local copies, waits for them, and re-layouts, local(): return jnp.transpose(out.reshape(block, 2, rows, total), (2, 1, 0, 3))  1.1 us
    transpose x1, local copies, waits for them, and re-layouts, local(): mine = jnp.transpose(vectors, (1, 2, 0, 3)).reshape(6, block, site_count)  0.95 us

profile of v2, /device:TPU:0, one launch (start us, length us, event | category | flops | bytes accessed | tf_op | source)
XLA Modules:
  0.0 47.1 jit_solution(10366101129752891666)
XLA Ops:
  0.0 0.9 %copy.4 = bf16[2,3,32,512]{3,2,1,0:T(8,128)(2,1)S(1)} copy(bf16[2,3,32,512]{3,0,1,2:T(2,128)(2,1)} %bitcast.8) | data formatting | bytes 393216 | tf_op jit(solution)/shard_map/transpose | solution.py:234
  1.0 0.0 copy-start
  1.0 0.0 copy-start.1
  1.0 0.6 %copy-done = s32[128]{0:T(128)S(1)} copy-done((s32[128]{0:T(128)S(1)}, s32[128]{0:T(128)}, u32[]{:S(2)}) %copy-start) | copy-done | bytes 536
  1.6 0.0 copy-done.1
  1.6 44.3 %shard_map.37 = f32[32,32,128]{2,1,0:T(8,128)S(1)} custom-call(s32[128]{0:T(128)S(1)} %copy-done, s32[3]{0:T(128)S(1)} %copy-done.1, bf16[6,32,512]{2,1,0:T(8,128)(2,1)S(1)} %bitcast.7), custom_call_target="tpu_custom_call" | custom-call | tf_op jit(solution)/shard_map/pallas_call | solution.py:236
  46.0 1.1 %copy.7 = f32[32,2,16,128]{3,0,1,2:T(8,128)} copy(f32[32,2,16,128]{3,2,1,0:T(8,128)S(1)} %bitcast.6) | data formatting | bytes 1048576 | tf_op jit(solution)/shard_map/reshape | solution.py:266
Async XLA Ops:
  1.0 0.7 %copy-start = (s32[128]{0:T(128)S(1)}, s32[128]{0:T(128)}, u32[]{:S(2)}) copy-start(s32[128]{0:T(128)} %slots_ref.1) | copy-start | bytes 1540
  1.0 0.7 %copy-start.1 = (s32[3]{0:T(128)S(1)}, s32[3]{0:T(128)}, u32[]{:S(2)}) copy-start(s32[3]{0:T(128)} %momentum_ref.1) | copy-start | bytes 40

commit v3 on v2

--- a/solution.py
+++ b/solution.py
@@ -130,15 +130,14 @@
         for c in range(6):
             wide[c, q * block : (q + 1) * block, :] = gathered[q, c].astype(jnp.float32)
 
-    order = [(2 * z + h) * rows for h in range(2) for z in range(planes)]
     for a in range(3):
-        real = wide[a]
-        imag = wide[3 + a]
-        first = [piece for i in order for piece in (real[i : i + rows], imag[i : i + rows])]
-        second = [piece for i in order for piece in (-imag[i : i + rows], real[i : i + rows])]
+        real = wide[a].T.astype(jnp.bfloat16)
+        imag = wide[3 + a].T.astype(jnp.bfloat16)
         low, high = a * site_count, (a + 1) * site_count
-        right[low:high] = jnp.concatenate(first, axis=0).T.astype(jnp.bfloat16)
-        right[span + low : span + high] = jnp.concatenate(second, axis=0).T.astype(jnp.bfloat16)
+        right[low:high, :total] = real
+        right[low:high, total:] = imag
+        right[span + low : span + high, :total] = -imag
+        right[span + low : span + high, total:] = real
 
     def fill(step):
         def one(half, carry):
@@ -199,15 +198,21 @@
 
     def body(step, carry):
         fill(step)
+
+        @pl.when(step >= 1)
+        def _():
+            forward(step - 1)
+
         product = jnp.dot(weighted[...], right[...], preferred_element_type=jnp.float32)
         for half in range(SLOTS):
             piece = product[half * total : (half + 1) * total].T
-            part[step, :, :, half] = piece.reshape(2, planes, 2 * rows, total)
+            for c in range(2):
+                for i in range(spaces):
+                    first = c * total + i * rows
+                    part[step, i % 2, i // 2, half, c * rows : (c + 1) * rows] = piece[
+                        first : first + rows
+                    ]
         pair_copy(step).start()
-
-        @pl.when(step >= 1)
-        def _():
-            forward(step - 1)
 
         return carry
 

time: 47.2 us -> 46.4 us (0.983)
  Pallas kernels: 44.3 us -> 43.6 us
    pallas_call x1, Pallas kernels: 44.3 us -> 43.6 us  [local(): pl.pallas_call(functools.partial(kernel, groups, spaces), out_shape=jax.S...]
where the time goes in v3:
time: 46.4 us; the launch traced here: 46.3 us
  Pallas kernels  43.6 us (94%)
  local copies, waits for them, and re-layouts  2.71 us (6%)
    pallas_call x1, Pallas kernels, local(): pl.pallas_call(functools.partial(kernel, groups, spaces), out_shape=jax.S...  43.6 us
    reshape x1, local copies, waits for them, and re-layouts, local(): return jnp.transpose(out.reshape(block, 2, rows, total), (2, 1, 0, 3))  1.1 us
    transpose x1, local copies, waits for them, and re-layouts, local(): mine = jnp.transpose(vectors, (1, 2, 0, 3)).reshape(6, block, site_count)  0.95 us

profile of v3, /device:TPU:0, one launch (start us, length us, event | category | flops | bytes accessed | tf_op | source)
XLA Modules:
  0.0 46.3 jit_solution(547293535288847980)
XLA Ops:
  0.0 0.9 %copy.4 = bf16[2,3,32,512]{3,2,1,0:T(8,128)(2,1)S(1)} copy(bf16[2,3,32,512]{3,0,1,2:T(2,128)(2,1)} %bitcast.8) | data formatting | bytes 393216 | tf_op jit(solution)/shard_map/transpose | solution.py:239
  1.0 0.0 copy-start
  1.0 0.0 copy-start.1
  1.0 0.6 %copy-done = s32[128]{0:T(128)S(1)} copy-done((s32[128]{0:T(128)S(1)}, s32[128]{0:T(128)}, u32[]{:S(2)}) %copy-start) | copy-done | bytes 536
  1.6 0.0 copy-done.1
  1.6 43.6 %shard_map.37 = f32[32,32,128]{2,1,0:T(8,128)S(1)} custom-call(s32[128]{0:T(128)S(1)} %copy-done, s32[3]{0:T(128)S(1)} %copy-done.1, bf16[6,32,512]{2,1,0:T(8,128)(2,1)S(1)} %bitcast.7), custom_call_target="tpu_custom_call" | custom-call | tf_op jit(solution)/shard_map/pallas_call | solution.py:241
  45.2 1.1 %copy.7 = f32[32,2,16,128]{3,0,1,2:T(8,128)} copy(f32[32,2,16,128]{3,2,1,0:T(8,128)S(1)} %bitcast.6) | data formatting | bytes 1048576 | tf_op jit(solution)/shard_map/reshape | solution.py:271
Async XLA Ops:
  1.0 0.7 %copy-start = (s32[128]{0:T(128)S(1)}, s32[128]{0:T(128)}, u32[]{:S(2)}) copy-start(s32[128]{0:T(128)} %slots_ref.1) | copy-start | bytes 1540
  1.0 0.7 %copy-start.1 = (s32[3]{0:T(128)S(1)}, s32[3]{0:T(128)}, u32[]{:S(2)}) copy-start(s32[3]{0:T(128)} %momentum_ref.1) | copy-start | bytes 40

commit v4 on v3

--- a/solution.py
+++ b/solution.py
@@ -27,6 +27,7 @@
     right,
     weighted,
     part,
+    pair_out,
     part_in,
     rounded,
     rounded_in,
@@ -139,7 +140,7 @@
         right[span + low : span + high, :total] = -imag
         right[span + low : span + high, total:] = real
 
-    def fill(step):
+    def fill(step, first, stop):
         def one(half, carry):
             k = slots_ref[group * block + SLOTS * step + half]
             row = [wide[c, pl.ds(k, 1), :] for c in range(6)]
@@ -166,11 +167,11 @@
 
             return lax.fori_loop(0, total // ROWS, tile, carry, unroll=True)
 
-        lax.fori_loop(0, SLOTS, one, 0)
+        lax.fori_loop(first, stop, one, 0)
 
     def pair_copy(step):
         return pltpu.make_async_remote_copy(
-            src_ref=part.at[step, 1 - core],
+            src_ref=pair_out.at[step],
             dst_ref=part_in.at[step],
             send_sem=pair_send.at[step],
             recv_sem=pair_recv.at[step],
@@ -191,18 +192,19 @@
 
     def forward(step):
         pair_copy(step).wait()
-        rounded[step] = (part[step, core] + part_in[step]).astype(jnp.bfloat16)
+        rounded[step] = (part[step, core] + part_in[step].astype(jnp.float32)).astype(jnp.bfloat16)
         for off in range(1, planes):
             sum_copy(step, off).start()
-        out_ref[pl.ds(SLOTS * step, SLOTS)] = part[step, core, plane] + part_in[step, plane]
+        out_ref[pl.ds(SLOTS * step, SLOTS)] = part[step, core, plane] + part_in[step, plane].astype(jnp.float32)
 
     def body(step, carry):
-        fill(step)
+        fill(step, 0, SLOTS - 1)
 
         @pl.when(step >= 1)
         def _():
             forward(step - 1)
 
+        fill(step, SLOTS - 1, SLOTS)
         product = jnp.dot(weighted[...], right[...], preferred_element_type=jnp.float32)
         for half in range(SLOTS):
             piece = product[half * total : (half + 1) * total].T
@@ -212,6 +214,7 @@
                     part[step, i % 2, i // 2, half, c * rows : (c + 1) * rows] = piece[
                         first : first + rows
                     ]
+        pair_out[step] = part[step, 1 - core].astype(jnp.bfloat16)
         pair_copy(step).start()
 
         return carry
@@ -253,7 +256,8 @@
             pltpu.VMEM((6 * site_count, 2 * total), jnp.bfloat16),
             pltpu.VMEM((SLOTS * total, 6 * site_count), jnp.bfloat16),
             pltpu.VMEM((steps, 2, planes, SLOTS, 2 * rows, total), jnp.float32),
-            pltpu.VMEM((steps, planes, SLOTS, 2 * rows, total), jnp.float32),
+            pltpu.VMEM((steps, planes, SLOTS, 2 * rows, total), jnp.bfloat16),
+            pltpu.VMEM((steps, planes, SLOTS, 2 * rows, total), jnp.bfloat16),
             pltpu.VMEM((steps, planes, SLOTS, 2 * rows, total), jnp.bfloat16),
             pltpu.VMEM((planes - 1, steps, SLOTS, 2 * rows, total), jnp.bfloat16),
             dma,

time: 46.4 us -> 46 us (level)
  no operation moved by 1% of the time
where the time goes in v4:
time: 46 us; the launch traced here: 45.9 us
  Pallas kernels  43.2 us (94%)
  local copies, waits for them, and re-layouts  2.71 us (6%)
    pallas_call x1, Pallas kernels, local(): pl.pallas_call(functools.partial(kernel, groups, spaces), out_shape=jax.S...  43.2 us
    reshape x1, local copies, waits for them, and re-layouts, local(): return jnp.transpose(out.reshape(block, 2, rows, total), (2, 1, 0, 3))  1.1 us
    transpose x1, local copies, waits for them, and re-layouts, local(): mine = jnp.transpose(vectors, (1, 2, 0, 3)).reshape(6, block, site_count)  0.95 us

profile of v4, /device:TPU:0, one launch (start us, length us, event | category | flops | bytes accessed | tf_op | source)
XLA Modules:
  0.0 45.9 jit_solution(14177122646241027564)
XLA Ops:
  0.0 0.9 %copy.4 = bf16[2,3,32,512]{3,2,1,0:T(8,128)(2,1)S(1)} copy(bf16[2,3,32,512]{3,0,1,2:T(2,128)(2,1)} %bitcast.8) | data formatting | bytes 393216 | tf_op jit(solution)/shard_map/transpose | solution.py:242
  1.0 0.0 copy-start
  1.0 0.0 copy-start.1
  1.0 0.6 %copy-done = s32[128]{0:T(128)S(1)} copy-done((s32[128]{0:T(128)S(1)}, s32[128]{0:T(128)}, u32[]{:S(2)}) %copy-start) | copy-done | bytes 536
  1.6 0.0 copy-done.1
  1.6 43.2 %shard_map.37 = f32[32,32,128]{2,1,0:T(8,128)S(1)} custom-call(s32[128]{0:T(128)S(1)} %copy-done, s32[3]{0:T(128)S(1)} %copy-done.1, bf16[6,32,512]{2,1,0:T(8,128)(2,1)S(1)} %bitcast.7), custom_call_target="tpu_custom_call" | custom-call | tf_op jit(solution)/shard_map/pallas_call | solution.py:244
  44.8 1.1 %copy.7 = f32[32,2,16,128]{3,0,1,2:T(8,128)} copy(f32[32,2,16,128]{3,2,1,0:T(8,128)S(1)} %bitcast.6) | data formatting | bytes 1048576 | tf_op jit(solution)/shard_map/reshape | solution.py:275
Async XLA Ops:
  1.0 0.7 %copy-start = (s32[128]{0:T(128)S(1)}, s32[128]{0:T(128)}, u32[]{:S(2)}) copy-start(s32[128]{0:T(128)} %slots_ref.1) | copy-start | bytes 1540
  1.0 0.7 %copy-start.1 = (s32[3]{0:T(128)S(1)}, s32[3]{0:T(128)}, u32[]{:S(2)}) copy-start(s32[3]{0:T(128)} %momentum_ref.1) | copy-start | bytes 40
